TPU v7x, 128 devices: a whole 4x4x4 slice. The times are simulated.
128 devices in a mesh: tx: 8 (over x, core), ty: 16 (over z, y).
Axes of the slice: x: 4, y: 4, z: 4, core: 2. Of those that a mesh axis runs over, the one named last changes fastest.
Arguments:
- solution: float32 [4, 1024, 4096], P(None, 'tx', 'ty'), may hold values from -6 to 6
- residual: float32 [4, 1024, 4096], P(None, 'tx', 'ty')
- direction: float32 [4, 1024, 4096], P(None, 'tx', 'ty')
- blocks: bfloat16 [32768, 128, 256], P(('tx', 'ty')), may hold values from -0.375 to 0.375
- bin_owner: int32 [32768, 1], P(('tx', 'ty')), may hold values from 0 to 127; in each aligned block of 256 rows (0 to 255, 256 to 511, ...) at most 3 rows name the same one
- bin_tile: int32 [32768], P(('tx', 'ty')), may hold values from 0 to 127
Outputs:
- next_solution: float32 [4, 1024, 4096], P(None, 'tx', 'ty')
- next_residual: float32 [4, 1024, 4096], P(None, 'tx', 'ty')
- next_direction: float32 [4, 1024, 4096], P(None, 'tx', 'ty')
Inputs may be any that keep to these rules, and one draw needn't show every extreme that they name: `bin_owner`: among the bins of one device, at most 3 name the same owner, and on some devices some owner is named by exactly 3 of them.
All inputs are finite; a program needn't handle non-finite values.
Results may differ from a plain program's by a relative error of at most 0.0024.
Values may be sent and summed in bfloat16 or wider, within the bound.
A program may use at most 128 MiB of HBM per device.

v0:
```python
import jax
import jax.numpy as jnp
from jax import lax
from jax.sharding import PartitionSpec as P

TILE_SIDE = 16


smooth_weight = 0.25


def padded_2(shard, sides, width):
    for axis, dim in sides:
        size, length = (lax.axis_size(axis), shard.shape[dim])
        up = [(i, (i + 1) % size) for i in range(size - 1)]
        down = [(j, i) for i, j in up]
        last = lax.slice_in_dim(shard, length - width, length, axis=dim)
        initial = lax.slice_in_dim(shard, 0, width, axis=dim)
        before = lax.ppermute(last, axis, up)
        after = lax.ppermute(initial, axis, down)
        shard = jnp.concatenate([before, shard, after], axis=dim)
    return shard


def to_tiles(field):
    beacons, rows, cols = field.shape
    across = rows // TILE_SIDE
    down = cols // TILE_SIDE
    shaped = field.reshape(beacons, across, TILE_SIDE, down, TILE_SIDE).transpose(1, 3, 0, 2, 4)
    return shaped.reshape(across * down, beacons, TILE_SIDE * TILE_SIDE)


def to_field(tiles, rows, cols):
    beacons = tiles.shape[1]
    across = rows // TILE_SIDE
    down = cols // TILE_SIDE
    shaped = tiles.reshape(across, down, beacons, TILE_SIDE, TILE_SIDE).transpose(2, 0, 3, 1, 4)
    return shaped.reshape(beacons, rows, cols)


def laplace_local(field):
    padded = padded_2(field.astype(jnp.bfloat16), (("tx", 1), ("ty", 2)), 1).astype(field.dtype)
    near = padded[:, 2:, 1:-1] + padded[:, :-2, 1:-1] + padded[:, 1:-1, 2:] + padded[:, 1:-1, :-2]
    return 4.0 * field - near


def per_device(solution, residual, direction, blocks, bin_owner, bin_tile):
    beacons, rows, cols = direction.shape
    cells = TILE_SIDE * TILE_SIDE
    across_x = lax.axis_size("tx")
    across_y = lax.axis_size("ty")
    devices = across_x * across_y
    count = blocks.shape[0]
    cap = max(2, 3 * count // (2 * devices))
    owner = bin_owner[:, 0]
    member = (owner[:, None] == jnp.arange(devices, dtype=jnp.int32)[None, :]).astype(jnp.int32)
    before = jnp.cumsum(member, axis=0) - member
    rank = jnp.sum(before * member, axis=1)
    slot = owner * cap + rank
    request = jnp.full((devices * cap,), -1, jnp.int32).at[slot].set(bin_tile)
    wanted = lax.all_to_all(
        request.reshape(devices, cap), ("tx", "ty"), split_axis=0, concat_axis=0, tiled=True
    )
    wanted = jnp.maximum(wanted.reshape(devices * cap), 0)
    own_tiles = to_tiles(direction.astype(jnp.bfloat16))
    outgoing = jnp.take(own_tiles, wanted, axis=0)
    fetched = lax.all_to_all(
        outgoing.reshape(devices, cap, beacons, cells),
        ("tx", "ty"),
        split_axis=0,
        concat_axis=0,
        tiled=True,
    )
    fetched = fetched.reshape(devices * cap, beacons, cells)
    picked = jnp.take(fetched, slot, axis=0)
    samples = jnp.einsum("bsc,bkc->bks", blocks, picked, preferred_element_type=jnp.float32).astype(
        jnp.bfloat16
    )
    adjoint = jnp.einsum("bsc,bks->bkc", blocks, samples, preferred_element_type=jnp.float32)
    returned = jnp.zeros((devices * cap, beacons, cells), jnp.float32).at[slot].set(adjoint)
    arrived = lax.all_to_all(
        returned.reshape(devices, cap, beacons, cells),
        ("tx", "ty"),
        split_axis=0,
        concat_axis=0,
        tiled=True,
    )
    arrived = arrived.reshape(devices * cap, beacons, cells)
    data_tiles = jnp.zeros(own_tiles.shape, jnp.float32).at[wanted].add(arrived)
    image = to_field(data_tiles, rows, cols) + smooth_weight * laplace_local(direction)
    norm_old = lax.psum(jnp.sum(residual * residual, axis=(1, 2)), ("tx", "ty"))
    curvature = lax.psum(jnp.sum(direction * image, axis=(1, 2)), ("tx", "ty"))
    alpha = norm_old / curvature
    next_residual = residual - alpha[:, None, None] * image
    norm_new = lax.psum(jnp.sum(next_residual * next_residual, axis=(1, 2)), ("tx", "ty"))
    next_solution = solution + alpha[:, None, None] * direction
    next_direction = next_residual + (norm_new / norm_old)[:, None, None] * direction
    return (next_solution, next_residual, next_direction)


def solution(mesh):
    placed = (
        P(None, "tx", "ty"),
        P(None, "tx", "ty"),
        P(None, "tx", "ty"),
        P(("tx", "ty"), None, None),
        P(("tx", "ty"), None),
        P(("tx", "ty")),
    )
    return jax.shard_map(
        per_device,
        mesh=mesh,
        in_specs=placed,
        out_specs=(P(None, "tx", "ty"), P(None, "tx", "ty"), P(None, "tx", "ty")),
        check_vma=False,
    )
```

profile of v0, /device:TPU:1, one launch (start us, length us, event | category | flops | bytes accessed | tf_op | source)
XLA Modules:
  0.0 293.7 jit_solution(3272720926653905522)
XLA Ops:
  3.3 1.6 scatter_custom_fusion
  5.7 11.5 %all-to-all-start = ((s32[128,1,3]{2,1,0:T(1,128)}), s32[128,1,3]{2,1,0:T(1,128)S(1)}, u32[]{:S(2)}, u32[]{:S(2)}) async-start(s32[128,1,3]{2,1,0:T(1,128)} %bitcast.7), calls=%async_computation | async-start | bytes 131072 | tf_op jit(solution)/shard_map/all_to_all | solution.py:61
  18.3 2.5 reshape.85
  20.7 2.1 copy.33
  22.9 2.0 reshape.86
  25.1 1.8 all-to-all-done
  27.7 2.3 gather_fusion
  30.1 1.4 broadcast_select_fusion
  31.4 8.0 %all-to-all-start.1 = ((bf16[128,3,4,256]{3,2,1,0:T(4,128)(2,1)}), bf16[128,3,4,256]{3,2,1,0:T(4,128)(2,1)S(1)}, u32[]{:S(2)}, u32[]{:S(2)}) async-start(bf16[128,3,4,256]{3,2,1,0:T(4,128)(2,1)} %broadcast_select_fusion), calls=%async_computation.1 | async-start | bytes 1572864 | tf_op jit(solution)/shard_map/all_to_all | solution.py:67
  39.4 16.7 %all-to-all-done.1 = bf16[128,3,4,256]{3,2,1,0:T(4,128)(2,1)S(1)} async-done(((bf16[128,3,4,256]{3,2,1,0:T(4,128)(2,1)}), bf16[128,3,4,256]{3,2,1,0:T(4,128)(2,1)S(1)}, u32[]{:S(2)}, u32[]{:S(2)}) %all-to-all-start.1) | async-done | bytes 786464 | tf_op jit(solution)/shard_map/all_to_all | solution.py:67
  57.3 16.9 %fusion = f32[256,4,256]{2,1,0:T(4,128)S(1)} fusion(bf16[256,128,256]{2,1,0:T(8,128)(2,1)} %param.9, bf16[256,4,256]{2,1,0:T(4,128)(2,1)S(1)} %gather_fusion.1, pred[256]{0:T(512)(128)(4,1)S(1)} %get-tuple-element.9), kind=kOutput, calls=%fused_computation.8 | convolution fusion | flops 134610944 | bytes 18350336 | tf_op jit(solution)/shard_map/bsc,bks->bkc/dot_general | solution.py:79
  75.5 24.0 %scatter_fusion = f32[384,4,256]{2,1,0:T(4,128)} fusion(f32[384,4,256]{2,1,0:T(4,128)} %broadcast_in_dim.38, s32[256]{0:T(256)S(1)} %bitcast.49, f32[256,4,256]{2,1,0:T(4,128)S(1)} %fusion), kind=kCustom, calls=%fused_computation.3 | custom fusion | bytes 3146752 | tf_op jit(solution)/shard_map/scatter | solution.py:80
  99.5 4.1 %all-to-all-start.2 = ((f32[128,3,4,256]{3,2,1,0:T(4,128)}), f32[128,3,4,256]{3,2,1,0:T(4,128)S(1)}, u32[]{:S(2)}, u32[]{:S(2)}) async-start(f32[128,3,4,256]{3,2,1,0:T(4,128)} %bitcast.12), calls=%async_computation.2 | async-start | bytes 3145728 | tf_op jit(solution)/shard_map/all_to_all | solution.py:81
  103.6 3.1 %collective-permute-start.1 = (bf16[4,1,256]{2,1,0:T(2,128)(2,1)S(1)}, bf16[4,1,256]{2,1,0:T(2,128)(2,1)S(1)}, u32[]{:S(2)}, u32[]{:S(2)}) collective-permute-start(bf16[4,1,256]{2,1,0:T(2,128)(2,1)S(1)} %get-tuple-element.16), channel_id=1, source_target_pairs={{16,0},{32,16},{48,32},{64,48},{80,64},{96,80},{112,96},{17,1},{33... | collective-permute-start | bytes 6152 | tf_op jit(solution)/shard_map/ppermute | solution.py:20
  106.7 2.4 collective-permute-start
  109.2 13.2 %collective-permute-done.1 = bf16[4,1,256]{2,1,0:T(2,128)(2,1)S(1)} collective-permute-done((bf16[4,1,256]{2,1,0:T(2,128)(2,1)S(1)}, bf16[4,1,256]{2,1,0:T(2,128)(2,1)S(1)}, u32[]{:S(2)}, u32[]{:S(2)}) %collective-permute-start.1) | collective-permute-done | bytes 2080 | tf_op jit(solution)/shard_map/ppermute | solution.py:20
  122.6 1.5 collective-permute-start.3
  124.1 4.0 %collective-permute-start.2 = (bf16[4,130,1]{2,1,0:T(8,128)(2,1)S(1)}, bf16[4,130,1]{2,1,0:T(8,128)(2,1)S(1)}, u32[]{:S(2)}, u32[]{:S(2)}) collective-permute-start(bf16[4,130,1]{2,1,0:T(8,128)(2,1)S(1)} %get-tuple-element.13), channel_id=1, source_target_pairs={{0,1},{1,2},{2,3},{3,4},{4,5},{5,6},{6,7},{7,8},{8,9},{9,10},{10,1... | collective-permute-start | bytes 3128 | tf_op jit(solution)/shard_map/ppermute | solution.py:19
  130.5 14.7 %scatter_fusion.1 = f32[128,4,256]{2,1,0:T(4,128)S(1)} fusion(f32[128,4,256]{2,1,0:T(4,128)S(1)} %broadcast_in_dim.36, s32[384]{0:T(512)S(1)} %reshape.126, f32[384,4,256]{2,1,0:T(4,128)S(1)} %bitcast.39), kind=kCustom, calls=%fused_computation.4 | custom fusion | flops 393216 | bytes 4720128 | tf_op jit(solution)/shard_map/scatter-add | solution.py:89
  145.3 2.6 reshape.90
  147.9 5.9 %copy.31 = f32[4,8,16,16,16]{4,3,2,1,0:T(8,128)} copy(f32[4,8,16,16,16]{4,2,3,1,0:T(8,128)} %bitcast.37) | data formatting | bytes 1048576 | tf_op jit(solution)/shard_map/transpose | solution.py:37
  153.8 3.6 %reshape.91 = f32[4,128,256]{2,1,0:T(8,128)S(1)} reshape(f32[4,8,16,16,16]{4,3,2,1,0:T(8,128)} %copy.31) | data formatting | bytes 1048576 | tf_op jit(solution)/shard_map/reshape | solution.py:38
  158.0 71.7 %all-reduce = (f32[4]{0:T(128)S(1)}, f32[4]{0:T(128)S(1)}) all-reduce(f32[4]{0:T(128)S(1)} %get-tuple-element.17, f32[4]{0:T(128)S(1)} %get-tuple-element.7), channel_id=1, replica_groups=mesh['tx'=8,'ty'=16] {'tx','ty'}, use_global_device_ids=true, to_apply=%region_1.2 | all-reduce | flops 8 | bytes 64 | tf_op jit(solution)/shard_map/psum | solution.py:91
  230.0 62.5 %psum.23 = f32[4]{0:T(128)S(1)} all-reduce(f32[4]{0:T(128)S(1)} %get-tuple-element.5), channel_id=1, replica_groups=mesh['tx'=8,'ty'=16] {'tx','ty'}, use_global_device_ids=true, to_apply=%region_11.12 | all-reduce | flops 4 | bytes 32 | tf_op jit(solution)/shard_map/psum | solution.py:95
  (45 shorter events, 12.7 us)
Async XLA Ops:
  5.7 21.2 %all-to-all-start = ((s32[128,1,3]{2,1,0:T(1,128)}), s32[128,1,3]{2,1,0:T(1,128)S(1)}, u32[]{:S(2)}, u32[]{:S(2)}) async-start(s32[128,1,3]{2,1,0:T(1,128)} %bitcast.7), calls=%async_computation | async-start | bytes 131072 | tf_op jit(solution)/shard_map/all_to_all | solution.py:61
  31.4 24.7 %all-to-all-start.1 = ((bf16[128,3,4,256]{3,2,1,0:T(4,128)(2,1)}), bf16[128,3,4,256]{3,2,1,0:T(4,128)(2,1)S(1)}, u32[]{:S(2)}, u32[]{:S(2)}) async-start(bf16[128,3,4,256]{3,2,1,0:T(4,128)(2,1)} %broadcast_select_fusion), calls=%async_computation.1 | async-start | bytes 1572864 | tf_op jit(solution)/shard_map/all_to_all | solution.py:67
  99.5 30.9 %all-to-all-start.2 = ((f32[128,3,4,256]{3,2,1,0:T(4,128)}), f32[128,3,4,256]{3,2,1,0:T(4,128)S(1)}, u32[]{:S(2)}, u32[]{:S(2)}) async-start(f32[128,3,4,256]{3,2,1,0:T(4,128)} %bitcast.12), calls=%async_computation.2 | async-start | bytes 3145728 | tf_op jit(solution)/shard_map/all_to_all | solution.py:81
  103.6 18.8 %collective-permute-start.1 = (bf16[4,1,256]{2,1,0:T(2,128)(2,1)S(1)}, bf16[4,1,256]{2,1,0:T(2,128)(2,1)S(1)}, u32[]{:S(2)}, u32[]{:S(2)}) collective-permute-start(bf16[4,1,256]{2,1,0:T(2,128)(2,1)S(1)} %get-tuple-element.16), channel_id=1, source_target_pairs={{16,0},{32,16},{48,32},{64,48},{80,64},{96,80},{112,96},{17,1},{33... | collective-permute-start | bytes 6152 | tf_op jit(solution)/shard_map/ppermute | solution.py:20
  106.7 15.7 %collective-permute-start = (bf16[4,1,256]{2,1,0:T(2,128)(2,1)S(1)}, bf16[4,1,256]{2,1,0:T(2,128)(2,1)S(1)}, u32[]{:S(2)}, u32[]{:S(2)}) collective-permute-start(bf16[4,1,256]{2,1,0:T(2,128)(2,1)S(1)} %get-tuple-element.15), channel_id=1, source_target_pairs={{0,16},{16,32},{32,48},{48,64},{64,80},{80,96},{96,112},{1,17},{17... | collective-permute-start | bytes 6152 | tf_op jit(solution)/shard_map/ppermute | solution.py:19
  122.6 6.1 %collective-permute-start.3 = (bf16[4,130,1]{2,1,0:T(8,128)(2,1)S(1)}, bf16[4,130,1]{2,1,0:T(8,128)(2,1)S(1)}, u32[]{:S(2)}, u32[]{:S(2)}) collective-permute-start(bf16[4,130,1]{2,1,0:T(8,128)(2,1)S(1)} %get-tuple-element.14), channel_id=1, source_target_pairs={{1,0},{2,1},{3,2},{4,3},{5,4},{6,5},{7,6},{8,7},{9,8},{10,9},{11,1... | collective-permute-start | bytes 3128 | tf_op jit(solution)/shard_map/ppermute | solution.py:20
  124.1 6.0 %collective-permute-start.2 = (bf16[4,130,1]{2,1,0:T(8,128)(2,1)S(1)}, bf16[4,130,1]{2,1,0:T(8,128)(2,1)S(1)}, u32[]{:S(2)}, u32[]{:S(2)}) collective-permute-start(bf16[4,130,1]{2,1,0:T(8,128)(2,1)S(1)} %get-tuple-element.13), channel_id=1, source_target_pairs={{0,1},{1,2},{2,3},{3,4},{4,5},{5,6},{6,7},{7,8},{8,9},{9,10},{10,1... | collective-permute-start | bytes 3128 | tf_op jit(solution)/shard_map/ppermute | solution.py:19
  153.8 3.6 %copy-start = (f32[4,128,256]{2,1,0:T(8,128)S(1)}, f32[4,128,256]{2,1,0:T(8,128)}, u32[]{:S(2)}) copy-start(f32[4,128,256]{2,1,0:T(8,128)} %param.8) | copy-start | bytes 1572868
  153.8 3.6 %copy-start.1 = (f32[4,128,256]{2,1,0:T(8,128)S(1)}, f32[4,128,256]{2,1,0:T(8,128)}, u32[]{:S(2)}) copy-start(f32[4,128,256]{2,1,0:T(8,128)} %param.7) | copy-start | bytes 1572868
  157.4 135.1 %copy-start.3 = (f32[4,128,256]{2,1,0:T(8,128)S(1)}, f32[4,128,256]{2,1,0:T(8,128)}, u32[]{:S(2)}) copy-start(f32[4,128,256]{2,1,0:T(8,128)} %param.6) | copy-start | bytes 1572868
  230.0 63.7 %copy-start.2 = (f32[4,128,256]{2,1,0:T(8,128)}, f32[4,128,256]{2,1,0:T(8,128)S(1)}, u32[]{:S(2)}) copy-start(f32[4,128,256]{2,1,0:T(8,128)S(1)} %get-tuple-element.6) | copy-start | bytes 1572868
where the time goes:
time: 295 us; the launch traced here: 294 us
  blocking collectives  134 us (45%)
  local copies, waits for them, and re-layouts  51.7 us (18%)
  starting transfers between devices  34.6 us (12%)
  waiting for transfers between devices  33.7 us (11%)
  other arithmetic  21.7 us (7%)
  matrix products  16.9 us (6%)
    psum x1, blocking collectives, per_device(): norm_old = lax.psum(jnp.sum(residual * residual, axis=(1, 2)), ('tx', 'ty'))  71.7 us
    psum x1, blocking collectives, per_device(): lax.psum(jnp.sum(next_residual * next_residual, axis=(1, 2)), ('tx', 'ty'))  62.5 us
    scatter x1, local copies, waits for them, and re-layouts, per_device(): jnp.zeros((devices * cap, beacons, cells), jnp.float32).at[slot]  24 us
    dot_general x1, matrix products, per_device(): jnp.einsum('bsc,bks->bkc', blocks, samples, preferred_element_type=jnp.fl...  16.9 us
    all_to_all x1, waiting for transfers between devices, per_device(): lax.all_to_all(outgoing.reshape(devices, cap, beacons, cells), ('tx', 'ty...  16.7 us
    scatter-add x1, other arithmetic, per_device(): data_tiles = jnp.zeros(own_tiles.shape, jnp.float32).at[wanted].add(arrived)  14.7 us
    ppermute x2, waiting for transfers between devices, padded_2(): after = lax.ppermute(initial, axis, down)  13.9 us
    all_to_all x1, starting transfers between devices, per_device(): lax.all_to_all(request.reshape(devices, cap), ('tx', 'ty'), split_axis=0,...  11.5 us
  transfers between devices with their start and end apart: 7, of which 5 were waited for; matrix products, arithmetic and copies ran while one was open for 3% of the time, Pallas kernels for 0%

commit v1 on v0

v1 whole, which is shorter than its diff:
```python
import functools

import jax
import jax.numpy as jnp
from jax import lax
from jax.experimental import pallas as pl
from jax.experimental.pallas import tpu as pltpu
from jax.sharding import PartitionSpec as P

MESH = pl.DeviceIdType.MESH
SIDE = 16
CELLS = 256
SLOTS = 3
GROUP = 16
F32 = jnp.float32
BF16 = jnp.bfloat16
smooth_weight = 0.25


def iota(shape, dim):
    return lax.broadcasted_iota(jnp.int32, shape, dim)


def nt_dot(a, b):
    return lax.dot_general(a, b, (((1,), (1,)), ((), ())), preferred_element_type=F32)


def dot(a, b):
    return jnp.dot(a, b, preferred_element_type=F32)


def swap_chunks(load_row, groups, lhs, rep, parts, write):
    rows = groups * SIDE
    keep = iota((rows, CELLS), 0) % SIDE == iota((rows, CELLS), 1) // SIDE
    for part in range(parts):
        for b in range(SIDE):
            row = load_row(b, part)
            wide = jnp.broadcast_to(row, (groups, SIDE, CELLS)).reshape(rows, CELLS)
            lhs[:, b * CELLS : (b + 1) * CELLS] = jnp.where(keep, wide, 0.0).astype(BF16)
        step = rows // 4

        def body(i, _):
            at = pl.ds(pl.multiple_of(i * step, step), step)
            write(part, i, at, dot(lhs[at, :], rep[...]))
            return 0

        lax.fori_loop(0, 4, body, 0)


def kernel(
    nx, ny, owner_ref, tile_ref, dir_hbm, res_hbm, blocks_hbm,
    img_ref, coef_ref,
    dirv, resv, blk, rep, lhs, tiles, req, reqr, table, slots, bits, turned,
    out, rcv, ret, retr, data, low, halo, halor, row, rowr,
    load_sem, blk_sem, slot_sem, req_sem, halo_sem, halor_sem,
    fetch_sem, fetchr_sem, back_sem, backr_sem, sum_sem,
):
    n = nx * ny
    groups = n // GROUP
    count = blk.shape[0]
    tx, ty = lax.axis_index("tx"), lax.axis_index("ty")
    me = tx * ny + ty

    def ahead(d):
        peer = (me + d) % n
        return (peer // ny, peer % ny)

    def behind(d):
        peer = (me + n - d) % n
        return (peer // ny, peer % ny)

    load_dir = pltpu.make_async_copy(dir_hbm, dirv, load_sem.at[0])
    load_dir.start()
    load_res = pltpu.make_async_copy(res_hbm, resv, load_sem.at[1])
    load_blk = pltpu.make_async_copy(blocks_hbm, blk, blk_sem)
    load_blk.start()
    load_res.start()

    barrier = pltpu.get_barrier_semaphore()

    def greet(d, _):
        pl.semaphore_signal(barrier, inc=1, device_id=ahead(d), device_id_type=MESH)
        return 0

    lax.fori_loop(1, n, greet, 0)

    away = (owner_ref[...] - me + n) % n
    member = jnp.broadcast_to(away, (n, count)) == iota((n, count), 0)
    earlier = (iota((count, count), 0) < iota((count, count), 1)).astype(F32).astype(BF16)
    rank = dot(member.astype(F32).astype(BF16), earlier)
    coded = jnp.where(member, jnp.where(rank == 0.0, 1.0, jnp.where(rank == 1.0, 2.0, 4.0)), 0.0)
    named = (jnp.broadcast_to(tile_ref[...], (n, count)) == iota((n, count), 0)).astype(F32).astype(BF16)
    asked = nt_dot(coded.astype(BF16), named).astype(jnp.int32)
    req[...] = asked.reshape(n, 1, n)
    number = iota((8, count), 1).astype(F32).astype(BF16)
    bins = jnp.zeros((8, n), F32)
    for s in range(SLOTS):
        pick = jnp.where(member & (rank == float(s)), 1.0, 0.0).astype(BF16)
        bins = jnp.where(iota((8, n), 0) == s, nt_dot(number, pick), bins)
    table[...] = bins.astype(jnp.int32)
    same = iota((CELLS, CELLS), 0) % SIDE == iota((CELLS, CELLS), 1) % SIDE
    for b in range(SIDE):
        here = same & (iota((CELLS, CELLS), 1) // SIDE == b)
        rep[b * CELLS : (b + 1) * CELLS, :] = here.astype(F32).astype(BF16)

    load_dir.wait()
    beacons, rows, cols = dirv.shape
    edge_lane = jnp.where(iota((8, cols), 0) == 0, cols - 1, 0)
    edge = ((iota((8, cols), 1) == edge_lane) & (iota((8, cols), 0) < 2)).astype(F32).astype(BF16)
    for k in range(beacons):
        halo[0, k : k + 1, :] = dirv[k, rows - 1 : rows, :]
        halo[1, k : k + 1, :] = dirv[k, 0:1, :]
        ends = nt_dot(edge, dirv[k].astype(BF16))
        halo[2, k : k + 1, :rows] = ends[0:1, :]
        halo[3, k : k + 1, :rows] = ends[1:2, :]

    pl.semaphore_wait(barrier, n - 1)

    def ask(d, _):
        pltpu.make_async_remote_copy(
            req.at[d], reqr.at[d], req_sem.at[0], req_sem.at[1], device_id=ahead(d), device_id_type=MESH
        ).start()
        return 0

    lax.fori_loop(1, n, ask, 0)
    reqr[0] = req[0]
    sides = (((tx + 1) % nx, ty), ((tx + nx - 1) % nx, ty), (tx, (ty + 1) % ny), (tx, (ty + ny - 1) % ny))
    edges = [
        pltpu.make_async_remote_copy(
            halo.at[i], halor.at[i], halo_sem.at[i], halor_sem.at[i], device_id=side, device_id_type=MESH
        )
        for i, side in enumerate(sides)
    ]
    for copy in edges:
        copy.start()
    to_scalar = pltpu.make_async_copy(table, slots, slot_sem)
    to_scalar.start()

    def direction_row(b, part):
        return dirv[...].reshape(beacons * rows // SIDE, SIDE, cols)[:, b : b + 1, :]

    def write_tiles(part, i, at, value):
        tiles[at, :] = value.astype(BF16)

    swap_chunks(direction_row, beacons * rows // SIDE, lhs, rep, 1, write_tiles)

    rest = pl.ds(1, n - 1)
    asking = pltpu.make_async_remote_copy(
        req.at[rest], reqr.at[rest], req_sem.at[0], req_sem.at[1], device_id=ahead(1), device_id_type=MESH
    )
    asking.wait_recv()

    slot_rows = GROUP * SIDE
    at_slot = iota((slot_rows, n), 0) % SIDE // beacons
    at_beacon = iota((slot_rows, n), 0) % beacons

    def fetch_copy(d):
        return pltpu.make_async_remote_copy(
            out.at[d], rcv.at[d], fetch_sem, fetchr_sem.at[d // GROUP], device_id=behind(d), device_id_type=MESH
        )

    def send_fetch(d, _):
        fetch_copy(d).start()
        return 0

    def serve(g, _):
        span = pl.ds(g * GROUP, GROUP)
        words = jnp.broadcast_to(reqr[span], (GROUP, SIDE, n)).reshape(slot_rows, n)
        bit = (lax.shift_right_logical(words, at_slot) & 1).astype(F32)
        bits[pl.ds(pl.multiple_of(g * slot_rows, slot_rows), slot_rows), :] = bit
        pick = jnp.concatenate(
            [jnp.where(at_beacon == k, bit, 0.0).astype(BF16) for k in range(beacons)], axis=1
        )
        out[span] = dot(pick, tiles[...]).astype(BF16).reshape(GROUP, SIDE, CELLS)

        @pl.when(g > 0)
        def _():
            lax.fori_loop(jnp.maximum((g - 1) * GROUP, 1), g * GROUP, send_fetch, 0)

        return 0

    lax.fori_loop(0, groups, serve, 0)
    rcv[0] = out[0]
    lax.fori_loop((groups - 1) * GROUP, n, send_fetch, 0)

    lane_beacon = iota((n, slot_rows), 1) % beacons

    def turn(g, _):
        span = pl.ds(pl.multiple_of(g * slot_rows, slot_rows), slot_rows)
        flipped = jnp.transpose(bits[span, :])
        for k in range(beacons):
            turned[g, k * n : (k + 1) * n, :] = jnp.where(lane_beacon == k, flipped, 0.0).astype(BF16)
        return 0

    lax.fori_loop(0, groups, turn, 0)

    to_scalar.wait()
    load_blk.wait()
    row_slot = iota((SIDE, rows), 0) // beacons

    def back_copy(d):
        return pltpu.make_async_remote_copy(
            ret.at[d], retr.at[d], back_sem, backr_sem.at[d // GROUP], device_id=ahead(d), device_id_type=MESH
        )

    def send_back(d, _):
        back_copy(d).start()
        return 0

    def bin_work(d):
        x = rcv[d]
        total = jnp.zeros((SIDE, CELLS), F32)
        for s in range(SLOTS):
            block = blk[jnp.clip(slots[s, d], 0, count - 1)]
            sample = nt_dot(x, block)
            sample = jnp.where(row_slot == s, sample, 0.0).astype(BF16)
            total = total + dot(sample, block)
        ret[d] = total.astype(BF16)

    for g in range(groups):
        first = g * GROUP + (1 if g == 0 else 0)
        span = pl.ds(first, (g + 1) * GROUP - first)
        pltpu.make_async_remote_copy(
            out.at[span], rcv.at[span], fetch_sem, fetchr_sem.at[g], device_id=behind(1), device_id_type=MESH
        ).wait_recv()

        def four(i, _):
            for u in range(4):
                bin_work(g * GROUP + i * 4 + u)
            return 0

        lax.fori_loop(0, GROUP // 4, four, 0)
        if g > 0:
            lax.fori_loop(max((g - 1) * GROUP, 1), g * GROUP, send_back, 0)
    retr[0] = ret[0]
    lax.fori_loop((groups - 1) * GROUP, n, send_back, 0)

    load_res.wait()
    for copy in edges:
        copy.wait()
    row_at, lane_at = iota((rows, cols), 0), iota((rows, cols), 1)
    diagonal = iota((rows, rows), 0) == iota((rows, rows), 1)
    spread = iota((2 * rows, cols), 0) // rows == iota((2 * rows, cols), 1) // (cols - 1)
    spread = spread & ((iota((2 * rows, cols), 1) == 0) | (iota((2 * rows, cols), 1) == cols - 1))
    spread = spread.astype(F32).astype(BF16)
    for k in range(beacons):
        field = dirv[k]
        above = jnp.where(tx > 0, halor[0, k : k + 1, :], 0.0)
        below = jnp.where(tx < nx - 1, halor[1, k : k + 1, :], 0.0)
        left = jnp.where(ty > 0, halor[2, k : k + 1, :rows], 0.0)
        right = jnp.where(ty < ny - 1, halor[3, k : k + 1, :rows], 0.0)
        ends = jnp.concatenate(
            [jnp.where(diagonal, left, 0.0).astype(BF16), jnp.where(diagonal, right, 0.0).astype(BF16)], axis=1
        )
        near = dot(ends, spread)
        near = near + jnp.where(row_at == 0, above, pltpu.roll(field, 1, 0))
        near = near + jnp.where(row_at == rows - 1, below, pltpu.roll(field, rows - 1, 0))
        near = near + jnp.where(lane_at == 0, 0.0, pltpu.roll(field, 1, 1))
        near = near + jnp.where(lane_at == cols - 1, 0.0, pltpu.roll(field, cols - 1, 1))
        img_ref[k] = smooth_weight * (4.0 * field - near)

    for g in range(groups):
        first = g * GROUP + (1 if g == 0 else 0)
        span = pl.ds(first, (g + 1) * GROUP - first)
        pltpu.make_async_remote_copy(
            ret.at[span], retr.at[span], back_sem, backr_sem.at[g], device_id=ahead(1), device_id_type=MESH
        ).wait_recv()
        part = dot(turned[g], retr[g * GROUP : (g + 1) * GROUP].reshape(slot_rows, CELLS))
        if g == 0:
            data[...] = part
        else:
            data[...] += part

    value = data[...]
    low[...] = value - value.astype(BF16).astype(F32)

    def data_row(b, part):
        source = data if part == 0 else low
        return source[...].reshape(beacons * rows // SIDE, SIDE, cols)[:, b : b + 1, :]

    def write_image(part, i, at, value):
        img_ref[i] = img_ref[i] + value

    swap_chunks(data_row, beacons * rows // SIDE, lhs, rep, 2, write_image)

    lane = iota((1, n), 1)
    line = jnp.zeros((1, n), F32)
    for k in range(beacons):
        image, field, old = img_ref[k], dirv[k], resv[k]
        top = jnp.maximum(jnp.max(jnp.abs(image), axis=(0, 1), keepdims=True), 1e-30)
        scaled = image * (1.0 / top)
        facts = (
            jnp.sum(old * old, axis=(0, 1), keepdims=True),
            jnp.sum(field * image, axis=(0, 1), keepdims=True),
            top,
            jnp.sum(old * scaled, axis=(0, 1), keepdims=True),
            jnp.sum(scaled * scaled, axis=(0, 1), keepdims=True),
        )
        for q, fact in enumerate(facts):
            line = jnp.where(lane == q * beacons + k, fact, line)
    row[0] = line
    rowr[0] = line

    def tell(d, _):
        pltpu.make_async_remote_copy(
            row.at[0], rowr.at[d], sum_sem.at[0], sum_sem.at[1], device_id=ahead(d), device_id_type=MESH
        ).start()
        return 0

    lax.fori_loop(1, n, tell, 0)

    asking.wait_send()
    for phase, sem in ((out, fetch_sem), (ret, back_sem)):
        pltpu.make_async_remote_copy(
            phase.at[rest], phase.at[rest], sem, sem, device_id=ahead(1), device_id_type=MESH
        ).wait_send()
    telling = pltpu.make_async_remote_copy(
        rowr.at[rest], rowr.at[rest], sum_sem.at[0], sum_sem.at[1], device_id=ahead(1), device_id_type=MESH
    )
    telling.wait_recv()
    lines = rowr[...].reshape(n, n)
    sums = jnp.sum(lines, axis=0, keepdims=True)
    alpha = sums / pltpu.roll(sums, n - beacons, 1)
    reach = alpha * pltpu.roll(lines, n - 2 * beacons, 1)
    cross = pltpu.roll(lines, n - 3 * beacons, 1)
    square = pltpu.roll(lines, n - 4 * beacons, 1)
    after = jnp.sum(lines - 2.0 * reach * cross + reach * reach * square, axis=0, keepdims=True)
    beta = after / sums
    coef_ref[...] = jnp.where(iota((8, n), 0) == 0, alpha, beta)
    telling.wait_send()


def per_device(nx, ny, solution, residual, direction, blocks, bin_owner, bin_tile):
    beacons, rows, cols = direction.shape
    count = blocks.shape[0]
    n = nx * ny
    groups = n // GROUP
    anyspace = pl.BlockSpec(memory_space=pl.ANY)
    vmem = pl.BlockSpec(memory_space=pltpu.VMEM)
    dma = pltpu.SemaphoreType.DMA
    image, coef = pl.pallas_call(
        functools.partial(kernel, nx, ny),
        out_shape=(
            jax.ShapeDtypeStruct((beacons, rows, cols), F32),
            jax.ShapeDtypeStruct((8, n), F32),
        ),
        in_specs=[vmem, vmem, anyspace, anyspace, anyspace],
        out_specs=(vmem, vmem),
        scratch_shapes=[
            pltpu.VMEM((beacons, rows, cols), F32),
            pltpu.VMEM((beacons, rows, cols), F32),
            pltpu.VMEM(blocks.shape, BF16),
            pltpu.VMEM((SIDE * CELLS, CELLS), BF16),
            pltpu.VMEM((beacons * rows, SIDE * CELLS), BF16),
            pltpu.VMEM((beacons * rows, CELLS), BF16),
            pltpu.VMEM((n, 1, n), jnp.int32),
            pltpu.VMEM((n, 1, n), jnp.int32),
            pltpu.VMEM((8, n), jnp.int32),
            pltpu.SMEM((8, n), jnp.int32),
            pltpu.VMEM((n * SIDE, n), F32),
            pltpu.VMEM((groups, beacons * n, GROUP * SIDE), BF16),
            pltpu.VMEM((n, SIDE, CELLS), BF16),
            pltpu.VMEM((n, SIDE, CELLS), BF16),
            pltpu.VMEM((n, SIDE, CELLS), BF16),
            pltpu.VMEM((n, SIDE, CELLS), BF16),
            pltpu.VMEM((beacons * rows, CELLS), F32),
            pltpu.VMEM((beacons * rows, CELLS), F32),
            pltpu.VMEM((4, 8, cols), F32),
            pltpu.VMEM((4, 8, cols), F32),
            pltpu.VMEM((1, 1, n), F32),
            pltpu.VMEM((n, 1, n), F32),
            dma((2,)),
            dma,
            dma,
            dma((2,)),
            dma((4,)),
            dma((4,)),
            dma,
            dma((groups,)),
            dma,
            dma((groups,)),
            dma((2,)),
        ],
        compiler_params=pltpu.CompilerParams(
            collective_id=0, has_side_effects=True, vmem_limit_bytes=60 * 1024 * 1024
        ),
        name="exchange",
    )(bin_owner.reshape(1, count), bin_tile.reshape(1, count), direction, residual, blocks)
    alpha = coef[0, :beacons, None, None]
    beta = coef[1, :beacons, None, None]
    next_residual = residual - alpha * image
    return solution + alpha * direction, next_residual, next_residual + beta * direction


def solution(mesh):
    field = P(None, "tx", "ty")
    placed = (field, field, field, P(("tx", "ty"), None, None), P(("tx", "ty"), None), P(("tx", "ty")))
    return jax.shard_map(
        functools.partial(per_device, mesh.shape["tx"], mesh.shape["ty"]),
        mesh=mesh,
        in_specs=placed,
        out_specs=(field, field, field),
        check_vma=False,
    )
```

time: 295 us -> 79.5 us (0.27)
  blocking collectives: 134 us -> 0 us
  Pallas kernels: 0 us -> 75.5 us
  local copies, waits for them, and re-layouts: 51.7 us -> 0.76 us
  starting transfers between devices: 34.6 us -> 0 us
  waiting for transfers between devices: 33.7 us -> 0 us
  other arithmetic: 21.7 us -> 2.37 us
  matrix products: 16.9 us -> 0 us
    psum x2 -> x0, blocking collectives: 134 us -> none  [the longest x1 71.7 us: per_device(): norm_old = lax.psum(jnp.sum(residual * residual, axis=(1, 2)), ('tx', 'ty'))]
    pallas_call x0 -> x1, Pallas kernels: none -> 75.5 us  [per_device(): pl.pallas_call(functools.partial(kernel, nx, ny), out_shape=(jax.ShapeDty...]
    scatter x2 -> x0, local copies, waits for them, and re-layouts: 25.5 us -> none  [the longest x1 24 us: per_device(): jnp.zeros((devices * cap, beacons, cells), jnp.float32).at[slot]]
    all_to_all x3 -> x0, starting transfers between devices: 23.5 us -> none  [the longest x1 11.5 us: per_device(): lax.all_to_all(request.reshape(devices, cap), ('tx', 'ty'), split_axis=0,...]
    all_to_all x3 -> x0, waiting for transfers between devices: 18.5 us -> none  [the longest x1 16.7 us: per_device(): lax.all_to_all(outgoing.reshape(devices, cap, beacons, cells), ('tx', 'ty...]
    dot_general x1 -> x0, matrix products: 16.9 us -> none  [per_device(): jnp.einsum('bsc,bks->bkc', blocks, samples, preferred_element_type=jnp.fl...]
    ppermute x4 -> x0, waiting for transfers between devices: 15.2 us -> none  [the longest x2 13.9 us: padded_2(): after = lax.ppermute(initial, axis, down)]
    scatter-add x1 -> x0, other arithmetic: 14.7 us -> none  [per_device(): data_tiles = jnp.zeros(own_tiles.shape, jnp.float32).at[wanted].add(arrived)]
  transfers between devices with their start and end apart: 7 -> 0, of which waited for: 5 -> 0; matrix products, arithmetic and copies ran while one was open for 3% -> 0% of each run, Pallas kernels for 0% -> 0%
where the time goes in v1:
time: 79.5 us; the launch traced here: 79.3 us
  Pallas kernels  75.5 us (95%)
  other arithmetic  2.37 us (3%)
    pallas_call x1, Pallas kernels, per_device(): pl.pallas_call(functools.partial(kernel, nx, ny), out_shape=(jax.ShapeDty...  75.5 us
    add x1, other arithmetic, per_device(): next_residual + beta * direction  2.37 us

profile of v1, /device:TPU:1, one launch (start us, length us, event | category | flops | bytes accessed | tf_op | source)
XLA Modules:
  0.0 79.3 jit_solution(6710067739192061282)
XLA Ops:
  0.6 0.0 copy-start
  0.6 0.0 copy-start.1
  0.7 0.0 copy-start.2
  0.7 75.5 %exchange.1 = (f32[4,128,256]{2,1,0:T(8,128)}, f32[8,128]{1,0:T(8,128)}) custom-call(s32[1,256]{1,0:T(1,128)} %bitcast.6, s32[1,256]{1,0:T(1,128)} %bitcast.7, f32[4,128,256]{2,1,0:T(8,128)} %dir_hbm.1, f32[4,128,256]{2,1,0:T(8,128)} %res_hbm.1, bf16[256,128,256]{2,1,0:T(8,128)(2,1)} %blocks_hbm.1), custom_call_target="tpu_custom_call" | custom-call | tf_op jit(solution)/shard_map/exchange/pallas_call | solution.py:341
  76.2 0.7 slice_bitcast_fusion
  77.0 0.0 copy-done
  77.0 0.0 copy-done.1
  77.0 0.0 copy-done.2
  77.0 2.4 %multiply_add_fusion = (f32[4,128,256]{2,1,0:T(8,128)}, f32[4,128,256]{2,1,0:T(8,128)}, f32[4,128,256]{2,1,0:T(8,128)}) fusion(f32[4,128,256]{2,1,0:T(8,128)S(1)} %copy-done, f32[4]{0:T(128)S(1)} %get-tuple-element.10, f32[4,128,256]{2,1,0:T(8,128)S(1)} %copy-done.1, f32[4,128,256]{2,1,0:T(8,128)} %get-tuple-element.6, f32[4]{0:T(128)S(1)} %get-tuple-element.11, ...), kind=kLoop, calls=%fused_computation | loop fusion | flops 786432 | bytes 3670048 | tf_op jit(solution)/shard_map/add | solution.py:392
Async XLA Ops:
  0.6 76.3 %copy-start = (f32[4,128,256]{2,1,0:T(8,128)S(1)}, f32[4,128,256]{2,1,0:T(8,128)}, u32[]{:S(2)}) copy-start(f32[4,128,256]{2,1,0:T(8,128)} %dir_hbm.1) | copy-start | bytes 1572868
  0.6 76.3 %copy-start.1 = (f32[4,128,256]{2,1,0:T(8,128)S(1)}, f32[4,128,256]{2,1,0:T(8,128)}, u32[]{:S(2)}) copy-start(f32[4,128,256]{2,1,0:T(8,128)} %res_hbm.1) | copy-start | bytes 1572868
  0.7 76.3 %copy-start.2 = (f32[4,128,256]{2,1,0:T(8,128)S(1)}, f32[4,128,256]{2,1,0:T(8,128)}, u32[]{:S(2)}) copy-start(f32[4,128,256]{2,1,0:T(8,128)} %param.6) | copy-start | bytes 1572868
